TPU v7x, 512 devices: a whole 4x4x16 slice. The times are simulated.
512 devices in a mesh: stack: 4 (over x), pix: 128 (over y, z, core).
Axes of the slice: x: 4, y: 4, z: 16, core: 2. Of those that a mesh axis runs over, the one named last changes fastest.
Arguments:
- slc: bfloat16 [2, 4, 15, 768, 256], P(None, 'stack', None, 'pix'), may hold values from -6 to 6
- owner_map: int32 [128], replicated, may hold values from 0 to 127, each once
Outputs:
- linked: float32 [2, 4, 15, 128, 1536], P(None, 'stack', None, 'pix')
- compressed: float32 [2, 4, 128, 1536], P(None, 'stack', 'pix')
Inputs may be any that keep to these rules, and one draw needn't show every extreme that they name: owner_map is a permutation: each owner slot receives exactly one column block.
All inputs are finite; a program needn't handle non-finite values.
Results may differ from a plain program's by a relative error of at most 0.005.
Values may be sent and summed in bfloat16 or wider, within the bound.
A program may use at most 64 MiB of HBM per device.

v0:
```python
import math

import jax
import jax.numpy as jnp
import numpy as np
from jax import lax
from jax.sharding import PartitionSpec as P

ITERS = 8


def padded_2(cells, sides, width):
    for axis, dim in sides:
        count = lax.axis_size(axis)
        ends = count - 1
        head = lax.slice_in_dim(cells, 0, width, axis=dim)
        tail = lax.slice_in_dim(cells, cells.shape[dim] - width, cells.shape[dim], axis=dim)
        cells = jnp.concatenate(
            [
                lax.ppermute(tail, axis, [(i, (i + 1) % count) for i in range(ends)]),
                cells,
                lax.ppermute(head, axis, [((i + 1) % count, i) for i in range(ends)]),
            ],
            axis=dim,
        )
    return cells


def shortened(x):

    def short(part):
        return part.astype(jnp.bfloat16) if part.dtype == jnp.float32 else part

    return jax.tree.map(short, x)


def shifted(block, axis, distance):
    devices = range(lax.axis_size(axis))
    route = [(i - distance, i) for i in devices if i - distance in devices]
    return lax.ppermute(block, axis, route)


def entering(x, axis, combine, identity):
    peers, here = (lax.axis_size(axis), lax.axis_index(axis))
    everything = jax.tree.map(lambda part: lax.all_gather(part, axis), x)
    start = jax.tree.map(
        lambda part, zero: jnp.broadcast_to(jnp.asarray(zero, part.dtype), part.shape), x, identity
    )

    def turn(k, before):
        reached = k < here
        new = combine(before, jax.tree.map(lambda part: part[k], everything))
        return jax.tree.map(lambda a, b: jnp.where(reached, a, b), new, before)

    return lax.fori_loop(0, peers, turn, start)


def window_sum(values, tall, broad):
    height = values.shape[-2] - tall + 1
    across = values[..., 0:height, :]
    for offset in range(1, tall):
        across = across + values[..., offset : offset + height, :]
    width = values.shape[-1] - broad + 1
    result = across[..., 0:width]
    for offset in range(1, broad):
        result = result + across[..., offset : offset + width]
    return result


def coherence(real_part, imag_part, tall, broad):
    dates = real_part.shape[0]
    first, second = np.triu_indices(dates, 1)
    groups = first.shape[0] // dates
    real_full = real_part.astype(jnp.float32)
    imag_full = imag_part.astype(jnp.float32)
    energy = window_sum(real_full * real_full + imag_full * imag_full, tall, broad) + 1.0

    def one_group(indices):
        left_idx, right_idx = indices
        left_re = real_full[left_idx]
        left_im = imag_full[left_idx]
        right_re = real_full[right_idx]
        right_im = imag_full[right_idx]
        prod_re = left_re * right_re + left_im * right_im
        prod_im = left_im * right_re - left_re * right_im
        scale = lax.rsqrt(energy[left_idx] * energy[right_idx])
        return (
            (window_sum(prod_re, tall, broad) * scale).astype(jnp.bfloat16),
            (window_sum(prod_im, tall, broad) * scale).astype(jnp.bfloat16),
        )

    first_groups = jnp.asarray(first.reshape(groups, dates), dtype=jnp.int32)
    second_groups = jnp.asarray(second.reshape(groups, dates), dtype=jnp.int32)
    gamma_re, gamma_im = lax.map(one_group, (first_groups, second_groups))
    return (
        gamma_re.reshape((-1,) + gamma_re.shape[2:]),
        gamma_im.reshape((-1,) + gamma_im.shape[2:]),
    )


def hermitian_tables(dates):
    first, second = np.triu_indices(dates, 1)
    npairs = first.shape[0]
    symmetric = np.zeros((dates * dates, npairs), np.float32)
    antisym = np.zeros((dates * dates, npairs), np.float32)
    for index in range(npairs):
        upper = int(first[index]) * dates + int(second[index])
        lower = int(second[index]) * dates + int(first[index])
        symmetric[upper, index] = 1.0
        symmetric[lower, index] = 1.0
        antisym[upper, index] = 1.0
        antisym[lower, index] = -1.0
    diagonal = np.eye(dates, dtype=np.float32).reshape(-1, 1)
    return (symmetric, antisym, diagonal)


def link_block(gamma_re, gamma_im, samples):
    dates = samples.shape[1]
    pixels = samples.shape[2]
    symmetric, antisym, diagonal = hermitian_tables(dates)
    full_re = (
        (
            jnp.dot(
                jnp.asarray(symmetric, dtype=jnp.bfloat16),
                gamma_re,
                preferred_element_type=jnp.float32,
            )
            + jnp.asarray(diagonal, dtype=jnp.float32)
        )
        .astype(jnp.bfloat16)
        .reshape(dates, dates, pixels)
    )
    full_im = (
        jnp.dot(
            jnp.asarray(antisym, dtype=jnp.bfloat16), gamma_im, preferred_element_type=jnp.float32
        )
        .astype(jnp.bfloat16)
        .reshape(dates, dates, pixels)
    )
    vec_re = jnp.ones((dates, pixels), jnp.float32)
    vec_im = jnp.zeros((dates, pixels), jnp.float32)
    for count in range(ITERS):
        next_re = jnp.sum(full_re * vec_re[None] - full_im * vec_im[None], axis=1)
        next_im = jnp.sum(full_re * vec_im[None] + full_im * vec_re[None], axis=1)
        energy = jnp.sum(next_re * next_re + next_im * next_im, axis=0) / dates
        factor = lax.rsqrt(energy + 0.25)
        vec_re = next_re * factor
        vec_im = next_im * factor
    sample_re = samples[0].astype(jnp.float32)
    sample_im = samples[1].astype(jnp.float32)
    norm = 1.0 / math.sqrt(dates)
    packed_re = jnp.sum(vec_re * sample_re + vec_im * sample_im, axis=0) * norm
    packed_im = jnp.sum(vec_re * sample_im - vec_im * sample_re, axis=0) * norm
    return (vec_re, vec_im, packed_re, packed_im)


def complex_product(earlier, later):
    return (
        earlier[0] * later[0] - earlier[1] * later[1],
        earlier[0] * later[1] + earlier[1] * later[0],
    )


def unit_link(later_re, later_im, earlier_re, earlier_im):
    link_re = later_re * earlier_re + later_im * earlier_im
    link_im = later_im * earlier_re - later_re * earlier_im
    factor = lax.rsqrt(link_re * link_re + link_im * link_im + 1.0)
    return (link_re * factor, link_im * factor)


def local(slc, owner_map):
    blocks = lax.axis_size("pix")
    dates = slc.shape[2]
    strip = slc.shape[3]
    columns = slc.shape[4]
    block_width = columns // blocks
    rows_all = strip * blocks
    pixels = rows_all * block_width
    inverse = jnp.argsort(owner_map)
    samples_here = slc[:, 0]
    padded = padded_2(samples_here, (("pix", 2),), 5)
    padded = jnp.pad(padded, ((0, 0), (0, 0), (0, 0), (2, 2)))
    strip_re, strip_im = coherence(padded[0], padded[1], 11, 5)

    def to_slots(values):
        feats = values.shape[0]
        grid = values.reshape(feats, strip, blocks, block_width)
        grid = jnp.take(grid, inverse, axis=2)
        return grid.transpose(2, 0, 1, 3).reshape(blocks, feats * strip * block_width)

    def from_slots(values, feats):
        grid = values.reshape(blocks, feats, strip, block_width)
        return grid.transpose(1, 3, 0, 2).reshape(feats, pixels)

    send_gamma = to_slots(jnp.concatenate([strip_re, strip_im], axis=0))
    send_samples = to_slots(samples_here.reshape(2 * dates, strip, columns))
    got_gamma, got_samples = (
        lax.all_to_all(
            shortened(send_gamma), "pix", split_axis=0, concat_axis=0, tiled=True
        ).astype(send_gamma.dtype),
        lax.all_to_all(send_samples, "pix", split_axis=0, concat_axis=0, tiled=True),
    )
    npairs = strip_re.shape[0]
    gamma_both = from_slots(got_gamma, 2 * npairs)
    gamma_re = gamma_both[:npairs]
    gamma_im = gamma_both[npairs:]
    owned = from_slots(got_samples, 2 * dates).reshape(2, dates, pixels)
    vec_re, vec_im, packed_re, packed_im = link_block(gamma_re, gamma_im, owned)
    packed = jnp.stack([packed_re, packed_im])
    following = shifted(packed, "stack", -1)
    unit_re, unit_im = unit_link(following[0], following[1], packed_re, packed_im)
    datum_re, datum_im = entering(
        (unit_re, unit_im),
        "stack",
        complex_product,
        (jnp.ones_like(unit_re), jnp.zeros_like(unit_re)),
    )
    linked_re = vec_re * datum_re[None] - vec_im * datum_im[None]
    linked_im = vec_re * datum_im[None] + vec_im * datum_re[None]
    linked = jnp.stack([linked_re, linked_im])[:, None, :, None, :]
    compressed = packed[:, None, None, :]
    return (linked, compressed)


def solution(mesh):
    in_specs = (P(None, "stack", None, "pix", None), P())
    out_specs = (P(None, "stack", None, "pix", None), P(None, "stack", "pix", None))
    return jax.shard_map(local, mesh=mesh, in_specs=in_specs, out_specs=out_specs, check_vma=False)
```

profile of v0, /device:TPU:6, one launch (start us, length us, event | category | flops | bytes accessed | tf_op | source)
XLA Modules:
  0.0 208.8 jit_solution(5926376294345217450)
XLA Ops:
  0.6 0.9 copy.52
  1.6 1.7 collective-permute-start
  3.3 1.3 collective-permute-start.1
  4.7 3.2 %sort.17 = (s32[128]{0:T(128)}, s32[128]{0:T(128)S(1)}) sort(s32[128]{0:T(128)} %param.12, s32[128]{0:T(128)S(1)} %iota.4), dimensions={0}, to_apply=%region_0.0 | sort | flops 896 | bytes 2048 | tf_op jit(solution)/shard_map/jit(argsort)/sort | solution.py:179
  7.8 1.9 copy.34
  10.2 1.7 gather_fusion.7
  13.3 0.6 reduce.7
  14.0 0.8 reshape.737
  14.8 24.4 %all-to-all-start.1 = ((bf16[128,2,180]{2,1,0:T(2,128)(2,1)}), bf16[128,2,180]{2,1,0:T(2,128)(2,1)}, u32[]{:S(2)}, u32[]{:S(2)}) async-start(bf16[128,2,180]{2,1,0:T(2,128)(2,1)} %reshape.737), calls=%async_computation.1 | async-start | bytes 262144 | tf_op jit(solution)/shard_map/all_to_all | solution.py:201
  40.1 39.5 %while.29 = (s32[]{:T(128)}, bf16[7,15,6,256]{3,2,1,0:T(8,128)(2,1)S(1)}, bf16[7,15,6,256]{3,2,1,0:T(8,128)(2,1)}, f32[15,16,260]{2,1,0:T(8,128)S(1)}, f32[15,16...) while((s32[]{:T(128)}, ...), condition=%wide.region_2.3_spmd.clone, body=%wide.region_1.2_spmd.sunk.clone.sunk | while | flops 1144060 | bytes 7716401 | solution.py:94
  40.1 0.7 fusion.34
  42.0 0.6 gather_fusion.2
  44.8 0.9 bitcast_dynamic-update-slice_fusion.3
  45.8 0.7 fusion.34
  50.5 0.9 bitcast_dynamic-update-slice_fusion.3
  51.4 0.7 fusion.34
  56.1 1.0 bitcast_dynamic-update-slice_fusion.3
  57.1 0.7 fusion.34
  61.7 1.0 bitcast_dynamic-update-slice_fusion.3
  62.7 0.7 fusion.34
  67.4 0.9 bitcast_dynamic-update-slice_fusion.3
  68.3 0.7 fusion.34
  73.0 1.0 bitcast_dynamic-update-slice_fusion.3
  74.0 0.7 fusion.34
  78.7 0.9 bitcast_dynamic-update-slice_fusion.3
  79.6 0.8 copy-done.2
  80.4 2.6 %copy.25 = bf16[7,15,6,256]{1,0,3,2:T(8,128)(2,1)S(1)} copy(bf16[7,15,6,256]{3,2,1,0:T(8,128)(2,1)} %copy-done.2) | data formatting | bytes 645120 | tf_op jit(solution)/shard_map/while | solution.py:94
  83.0 1.9 concatenate.12
  84.9 2.6 %copy.26 = bf16[7,15,6,256]{1,0,3,2:T(8,128)(2,1)S(1)} copy(bf16[7,15,6,256]{3,2,1,0:T(8,128)(2,1)} %get-tuple-element.158) | data formatting | bytes 645120 | tf_op jit(solution)/shard_map/while | solution.py:94
  87.6 2.6 %concatenate.13 = bf16[105,6,128,2]{0,3,2,1:T(2,128)(2,1)} reshape(bf16[7,15,6,256]{1,0,3,2:T(8,128)(2,1)S(1)} %copy.26) | data formatting | bytes 645120 | tf_op jit(solution)/shard_map/concatenate | solution.py:195
  90.2 2.5 %pad_maximum_fusion = bf16[210,6,128,2]{0,3,2,1:T(2,128)(2,1)S(1)} fusion(bf16[105,6,128,2]{0,3,2,1:T(2,128)(2,1)} %concatenate.13, bf16[105,6,128,2]{0,3,2,1:T(2,128)(2,1)S(1)} %concatenate.12), kind=kLoop, calls=%fused_computation.93 | loop fusion | flops 1290240 | bytes 1290240 | tf_op jit(solution)/shard_map/concatenate | solution.py:195
  92.7 2.4 %gather_fusion.6 = bf16[128,210,6,2]{1,3,2,0:T(2,128)(2,1)S(1)} fusion(bf16[210,6,128,2]{0,3,2,1:T(2,128)(2,1)S(1)} %pad_maximum_fusion, s32[1024]{0:T(1024)S(1)} %pad_clamp_fusion.2), kind=kCustom, calls=%fused_computation.6 | custom fusion | bytes 1290752 | tf_op jit(solution)/shard_map/jit(_take)/gather | solution.py:188
  95.1 0.8 broadcast_select_fusion
  95.9 1.7 copy.27
  97.6 1.0 reduce.6
  98.9 1.5 reshape.735
  100.5 15.9 %all-to-all-start = ((bf16[128,2,1260]{2,1,0:T(2,128)(2,1)}), bf16[128,2,1260]{2,1,0:T(2,128)(2,1)S(1)}, u32[]{:S(2)}, u32[]{:S(2)}) async-start(bf16[128,2,1260]{2,1,0:T(2,128)(2,1)} %reshape.735), calls=%async_computation | async-start | bytes 1310720 | tf_op jit(solution)/shard_map/all_to_all | solution.py:198
  116.4 1.1 reshape.738
  118.0 37.2 %all-to-all-done = bf16[128,2,1260]{2,1,0:T(2,128)(2,1)S(1)} async-done(((bf16[128,2,1260]{2,1,0:T(2,128)(2,1)}), bf16[128,2,1260]{2,1,0:T(2,128)(2,1)S(1)}, u32[]{:S(2)}, u32[]{:S(2)}) %all-to-all-start) | async-done | bytes 645152 | tf_op jit(solution)/shard_map/all_to_all | solution.py:198
  155.2 1.1 reshape.736
  156.3 1.5 copy.29
  157.9 1.2 fusion.27
  160.3 1.4 copy.31
  161.9 1.5 fusion.10
  163.4 1.5 reshape.662
  164.9 0.7 subtract_reduce_fusion.7
  165.7 0.7 subtract_reduce_fusion.6
  166.5 0.7 subtract_reduce_fusion.5
  167.4 0.7 subtract_reduce_fusion.4
  168.2 0.7 subtract_reduce_fusion.3
  169.0 0.7 subtract_reduce_fusion.2
  169.8 0.7 subtract_reduce_fusion.1
  170.6 1.4 subtract_reduce_fusion
  172.0 1.2 copy.33
  173.2 1.0 add_reduce_fusion.8
  174.2 1.2 copy.39
  175.4 0.8 rsqrt.76
  176.4 2.2 %fusion.14 = (f32[2,128,6]{2,1,0:T(8,128)S(1)}, f32[2,128,6]{2,1,0:T(8,128)S(1)}) fusion(f32[15,2,128,6]{0,3,2,1:T(8,128)S(1)} %reduce_sum.268, f32[15,2,128,6]{0,3,2,1:T(8,128)S(1)} %reduce_sum.267, f32[2,128,6]{2,1,0:T(8,128)} %rsqrt.76, bf16[30,2,128,6]{0,3,2,1:T(8,128)(2,1)S(1)} %bitcast.87), kind=kLoop, calls=%fused_computation.90 | loop fusion | flops 273408 | bytes 294912 | tf_op jit(solution)/shard_map/reduce_sum | solution.py:152
  178.9 2.7 %collective-permute-start.2 = (f32[2,1536]{1,0:T(2,128)S(1)}, f32[2,1536]{1,0:T(2,128)S(1)}, u32[]{:S(2)}, u32[]{:S(2)}) collective-permute-start(f32[2,1536]{1,0:T(2,128)S(1)} %get-tuple-element.273), channel_id=1, source_target_pairs={{128,0},{256,128},{384,256},{129,1},{257,129},{385,257},{130,2},{2... | collective-permute-start | bytes 36872 | tf_op jit(solution)/shard_map/ppermute | solution.py:40
  181.7 0.6 copy.41
  182.3 0.8 collective-permute-done.2
  183.1 12.1 %all-gather = f32[4,1,1536]{2,1,0:T(1,128)S(1)} all-gather(f32[1,1,1536]{2,1,0:T(1,128)S(1)} %multiply_bitcast_fusion.1), channel_id=1, replica_groups=mesh['stack'=4,'pix'=128] {'stack'}, dimensions={0}, use_global_device_ids=true | all-gather | bytes 30720 | tf_op jit(solution)/shard_map/all_gather | solution.py:45
  195.3 11.9 %all-gather.1 = f32[4,1,1536]{2,1,0:T(1,128)S(1)} all-gather(f32[1,1,1536]{2,1,0:T(1,128)S(1)} %get-tuple-element.251), channel_id=1, replica_groups=mesh['stack'=4,'pix'=128] {'stack'}, dimensions={0}, use_global_device_ids=true | all-gather | bytes 30720 | tf_op jit(solution)/shard_map/all_gather | solution.py:45
  208.0 0.9 copy.40
  (160 shorter events, 33.7 us)
Async XLA Ops:
  1.6 37.6 %collective-permute-start = (bf16[2,15,5,256]{3,2,1,0:T(8,128)(2,1)S(1)}, bf16[2,15,5,256]{3,2,1,0:T(8,128)(2,1)S(1)}, u32[]{:S(2)}, u32[]{:S(2)}) collective-permute-start(bf16[2,15,5,256]{3,2,1,0:T(8,128)(2,1)S(1)} %get-tuple-element.270), channel_id=1, source_target_pairs={{0,1},{1,2},{2,3},{3,4},{4,5},{5,6},{6,7},{7,8},{8,9},{9,10},{10,1... | collective-permute-start | bytes 230408 | tf_op jit(solution)/shard_map/ppermute | solution.py:20
  3.3 35.9 %collective-permute-start.1 = (bf16[2,15,5,256]{3,2,1,0:T(8,128)(2,1)S(1)}, bf16[2,15,5,256]{3,2,1,0:T(8,128)(2,1)S(1)}, u32[]{:S(2)}, u32[]{:S(2)}) collective-permute-start(bf16[2,15,5,256]{3,2,1,0:T(8,128)(2,1)S(1)} %get-tuple-element.271), channel_id=1, source_target_pairs={{1,0},{2,1},{3,2},{4,3},{5,4},{6,5},{7,6},{8,7},{9,8},{10,9},{11,1... | collective-permute-start | bytes 230408 | tf_op jit(solution)/shard_map/ppermute | solution.py:22
  14.8 85.7 %all-to-all-start.1 = ((bf16[128,2,180]{2,1,0:T(2,128)(2,1)}), bf16[128,2,180]{2,1,0:T(2,128)(2,1)}, u32[]{:S(2)}, u32[]{:S(2)}) async-start(bf16[128,2,180]{2,1,0:T(2,128)(2,1)} %reshape.737), calls=%async_computation.1 | async-start | bytes 262144 | tf_op jit(solution)/shard_map/all_to_all | solution.py:201
  79.6 0.8 copy-start.2
  100.5 54.8 %all-to-all-start = ((bf16[128,2,1260]{2,1,0:T(2,128)(2,1)}), bf16[128,2,1260]{2,1,0:T(2,128)(2,1)S(1)}, u32[]{:S(2)}, u32[]{:S(2)}) async-start(bf16[128,2,1260]{2,1,0:T(2,128)(2,1)} %reshape.735), calls=%async_computation | async-start | bytes 1310720 | tf_op jit(solution)/shard_map/all_to_all | solution.py:198
  157.9 1.8 copy-start.4
  157.9 1.8 copy-start.5
  160.3 1.6 copy-start.3
  178.6 29.0 %copy-start = (f32[15,1536]{1,0:T(8,128)S(1)}, f32[15,1536]{1,0:T(8,128)}, u32[]{:S(2)}) copy-start(f32[15,1536]{1,0:T(8,128)} %get-tuple-element.209) | copy-start | bytes 276484
  178.6 29.0 %copy-start.1 = (f32[15,1536]{1,0:T(8,128)S(1)}, f32[15,1536]{1,0:T(8,128)}, u32[]{:S(2)}) copy-start(f32[15,1536]{1,0:T(8,128)} %get-tuple-element.210) | copy-start | bytes 276484
  178.9 4.1 %collective-permute-start.2 = (f32[2,1536]{1,0:T(2,128)S(1)}, f32[2,1536]{1,0:T(2,128)S(1)}, u32[]{:S(2)}, u32[]{:S(2)}) collective-permute-start(f32[2,1536]{1,0:T(2,128)S(1)} %get-tuple-element.273), channel_id=1, source_target_pairs={{128,0},{256,128},{384,256},{129,1},{257,129},{385,257},{130,2},{2... | collective-permute-start | bytes 36872 | tf_op jit(solution)/shard_map/ppermute | solution.py:40
where the time goes:
time: 212 us; the launch traced here: 209 us
  local copies, waits for them, and re-layouts  61.7 us (29%)
  starting transfers between devices  46.1 us (22%)
  waiting for transfers between devices  38 us (18%)
  other arithmetic  35.1 us (17%)
  blocking collectives  24 us (11%)
    all_to_all x1, waiting for transfers between devices, local(): lax.all_to_all(shortened(send_gamma), 'pix', split_axis=0, concat_axis=0,...  37.2 us
    all_to_all x1, starting transfers between devices, local(): lax.all_to_all(send_samples, 'pix', split_axis=0, concat_axis=0, tiled=True)  24.4 us
    all_gather x2, blocking collectives, entering(): everything = jax.tree.map(lambda part: lax.all_gather(part, axis), x)  24 us
    all_to_all x1, starting transfers between devices, local(): lax.all_to_all(shortened(send_gamma), 'pix', split_axis=0, concat_axis=0,...  15.9 us
    unnamed x24, local copies, waits for them, and re-layouts  9.98 us
    gather x14, local copies, waits for them, and re-layouts, one_group(): scale = lax.rsqrt(energy[left_idx] * energy[right_idx])  7.89 us
    dynamic_update_slice x7, other arithmetic, coherence(): gamma_re, gamma_im = lax.map(one_group, (first_groups, second_groups))  6.66 us
    reduce_sum x8, other arithmetic, link_block(): next_re = jnp.sum(full_re * vec_re[None] - full_im * vec_im[None], axis=1)  6.5 us
  transfers between devices with their start and end apart: 5, of which 2 were waited for; matrix products, arithmetic and copies ran while one was open for 35% of the time, Pallas kernels for 0%

commit v1 on v0

v1 whole, which is shorter than its diff:
```python
import math

import jax
import jax.numpy as jnp
from jax import lax
from jax.experimental import pallas as pl
from jax.experimental.pallas import tpu as pltpu
from jax.sharding import PartitionSpec as P

MESH = pl.DeviceIdType.MESH
F32, BF16, I32 = jnp.float32, jnp.bfloat16, jnp.int32
DATES, ITERS, SECT, ROWS, COLS, BLOCKS = 15, 8, 4, 768, 256, 128
STRIP = 6
UP = 5
TALL = 16
NY, NZ, NC = 4, 16, 2
GROUPS = NY * NC
FEAT = 32
XS = 24
NT_DIMS = (((1,), (1,)), ((), ()))


def place(y, z, c):
    return y * (NZ * NC) + z * NC + c


def halo_kernel(x_ref, out_ref, send_sem, recv_sem):
    me = lax.axis_index("pix")
    count = BLOCKS
    after, before = lax.rem(me + 1, count), lax.rem(me + count - 1, count)
    barrier = pltpu.get_barrier_semaphore()
    for peer in (after, before):
        pl.semaphore_signal(barrier, inc=1, device_id={"pix": peer}, device_id_type=MESH)
    pl.semaphore_wait(barrier, 2)
    copies = []
    for i, peer in enumerate((after, before)):
        copy = pltpu.make_async_remote_copy(
            src_ref=x_ref,
            dst_ref=out_ref.at[i],
            send_sem=send_sem.at[i],
            recv_sem=recv_sem.at[i],
            device_id={"pix": peer},
            device_id_type=MESH,
        )
        copy.start()
        copies.append(copy)
    for copy in copies:
        copy.wait()


def exchange_halo(x):
    return pl.pallas_call(
        halo_kernel,
        out_shape=jax.ShapeDtypeStruct((2,) + x.shape, x.dtype),
        in_specs=[pl.BlockSpec(memory_space=pl.ANY)],
        out_specs=pl.BlockSpec(memory_space=pl.ANY),
        scratch_shapes=[pltpu.SemaphoreType.DMA((2,)), pltpu.SemaphoreType.DMA((2,))],
        compiler_params=pltpu.CompilerParams(collective_id=0, has_side_effects=True),
        name="halo",
    )(x)


def iota(shape, dim):
    return lax.broadcasted_iota(I32, shape, dim)


def one_hot(mask):
    return jnp.where(mask, 1.0, 0.0).astype(BF16)


def unpack(src_ref, plain, k):
    for t in range(DATES):
        for r in range(STRIP):
            pair = src_ref[t, r].astype(F32)
            row = (t * STRIP + r) * 2
            plain[k, 0, pl.ds(row, 2)] = pair[:, :128]
            plain[k, 1, pl.ds(row, 2)] = pair[:, 128:]


def spread(plain, k, r, row, x_ref, keep):
    for h in range(2):
        for comp in range(2):
            v = plain[k, h, pl.ds(r * 2 + comp, DATES, stride=STRIP * 2)]
            if keep is not None:
                v = jnp.where(keep, v, 0.0)
            x_ref[comp, h, pl.ds(row * XS, DATES)] = v
            x_ref[comp, h, pl.ds(row * XS + DATES, 8)] = v[:8]


def row_sums(terms):
    total = terms(10)
    for row in range(9, 4, -1):
        total = total + terms(row)
    sums = [None] * STRIP
    sums[5] = total
    for row in range(4, -1, -1):
        total = total + terms(row)
        sums[row] = total
    tail = None
    for r in range(1, STRIP):
        term = terms(r + 10)
        tail = term if tail is None else tail + term
        sums[r] = sums[r] + tail
    return sums


def pair_sums(terms):
    a, b = [], []

    def add(x, y):
        return (x[0] + y[0], x[1] + y[1])

    total = terms(10)
    for row in range(9, 4, -1):
        total = add(total, terms(row))
    sums = [None] * STRIP
    sums[5] = total
    for row in range(4, -1, -1):
        total = add(total, terms(row))
        sums[row] = total
    tail = None
    for r in range(1, STRIP):
        term = terms(r + 10)
        tail = term if tail is None else add(tail, term)
        sums[r] = add(sums[r], tail)
    return sums


def split_store(ref, lead, row, h, value):
    high = value.astype(BF16)
    low = (value - high.astype(F32)).astype(BF16)
    ref[lead, pl.ds(row, 16), h * 128 : (h + 1) * 128] = high
    ref[lead, pl.ds(row, 16), 256 + h * 128 : 256 + (h + 1) * 128] = low


def coherences(x_ref, sums_ref, band_ref, scale_ref, g_ref):
    band_ref[...] = one_hot(
        jnp.abs((iota((512, 256), 0) & 255) - iota((512, 256), 1)) <= 2
    )
    for h in range(2):

        def power(row):
            re = x_ref[0, h, pl.ds(row * XS, 16)]
            im = x_ref[1, h, pl.ds(row * XS, 16)]
            return re * re + im * im

        for r, value in enumerate(row_sums(power)):
            split_store(sums_ref, 0, r * 16, h, value)
    energy = jnp.dot(sums_ref[0, :96], band_ref[...], preferred_element_type=F32) + 1.0
    scale = lax.rsqrt(energy)
    for h in range(2):
        for r in range(STRIP):
            v = scale[r * 16 : (r + 1) * 16, h * 128 : (h + 1) * 128]
            scale_ref[h, pl.ds(r * XS, 16)] = v
            scale_ref[h, pl.ds(r * XS + DATES, 8)] = v[:8]
    for d in range(1, 8):
        for h in range(2):

            def product(row):
                are = x_ref[0, h, pl.ds(row * XS, 16)]
                aim = x_ref[1, h, pl.ds(row * XS, 16)]
                bre = x_ref[0, h, pl.ds(row * XS + d, 16)]
                bim = x_ref[1, h, pl.ds(row * XS + d, 16)]
                return (are * bre + aim * bim, aim * bre - are * bim)

            for r, pair in enumerate(pair_sums(product)):
                for part in range(2):
                    split_store(sums_ref, d, r * 32 + part * 16, h, pair[part])
        summed = jnp.dot(sums_ref[d], band_ref[...], preferred_element_type=F32)
        for h in range(2):
            for r in range(STRIP):
                both = scale_ref[h, pl.ds(r * XS, 16)] * scale_ref[h, pl.ds(r * XS + d, 16)]
                for part in range(2):
                    row = r * 32 + part * 16
                    v = summed[row : row + 16, h * 128 : (h + 1) * 128] * both
                    v = v.astype(BF16).astype(F32)
                    base = ((d - 1) * 2 + part) * 128
                    g_ref[h, pl.ds(base + r, 16, stride=8)] = v


def power_iterations(g_ref, plain, v_ref, c_ref, here):
    def entry(h, a, b):
        d = (b - a) % DATES
        flip = d > 7
        if flip:
            a, d = b, DATES - d
        base = (d - 1) * 256 + a * 8
        re = g_ref[h, pl.ds(base, STRIP)]
        im = g_ref[h, pl.ds(base + 128, STRIP)]
        return re, im, flip

    def normalized(parts):
        energy = None
        for re, im in parts:
            term = re * re + im * im
            energy = term if energy is None else energy + term
        factor = lax.rsqrt(energy * (1.0 / DATES) + 0.25)
        return tuple((re * factor, im * factor) for re, im in parts)

    def half(h, _):
        first = []
        for a in range(DATES):
            re, im = jnp.ones((STRIP, 128), F32), jnp.zeros((STRIP, 128), F32)
            for b in range(DATES):
                if b != a:
                    gre, gim, flip = entry(h, a, b)
                    re = re + gre
                    im = im - gim if flip else im + gim
            first.append((re, im))
        vec = normalized(first)

        def step(_, vec):
            out = []
            for a in range(DATES):
                re, im = vec[a]
                for b in range(DATES):
                    if b != a:
                        gre, gim, flip = entry(h, a, b)
                        vre, vim = vec[b]
                        if flip:
                            re = re + (gre * vre + gim * vim)
                            im = im + (gre * vim - gim * vre)
                        else:
                            re = re + (gre * vre - gim * vim)
                            im = im + (gre * vim + gim * vre)
                out.append((re, im))
            return normalized(out)

        vec = lax.fori_loop(0, ITERS - 1, step, vec)
        packed_re, packed_im = None, None
        for t in range(DATES):
            vre, vim = vec[t]
            sre = plain[0, h, pl.ds(t * STRIP * 2, STRIP, stride=2)]
            sim = plain[0, h, pl.ds(t * STRIP * 2 + 1, STRIP, stride=2)]
            re = vre * sre + vim * sim
            im = vre * sim - vim * sre
            packed_re = re if packed_re is None else packed_re + re
            packed_im = im if packed_im is None else packed_im + im
            v_ref[h, pl.ds(t * 8, STRIP)] = vre
            v_ref[h, pl.ds((16 + t) * 8, STRIP)] = vim
        norm = 1.0 / math.sqrt(DATES)
        packed_re, packed_im = packed_re * norm, packed_im * norm
        v_ref[h, pl.ds(15 * 8, STRIP)] = packed_re
        v_ref[h, pl.ds(31 * 8, STRIP)] = packed_im
        c_ref[here, 0, h] = packed_re
        c_ref[here, 1, h] = packed_im
        return 0

    lax.fori_loop(0, 2, half, 0)


def connect(v_ref, c_ref, here):
    for h in range(2):
        datum_re, datum_im = jnp.ones((STRIP, 128), F32), jnp.zeros((STRIP, 128), F32)
        for j in range(SECT - 1):
            ere, eim = c_ref[j, 0, h], c_ref[j, 1, h]
            lre, lim = c_ref[j + 1, 0, h], c_ref[j + 1, 1, h]
            link_re = lre * ere + lim * eim
            link_im = lim * ere - lre * eim
            factor = lax.rsqrt(link_re * link_re + link_im * link_im + 1.0)
            ure, uim = link_re * factor, link_im * factor
            new_re = datum_re * ure - datum_im * uim
            new_im = datum_re * uim + datum_im * ure
            reached = j < here
            datum_re = jnp.where(reached, new_re, datum_re)
            datum_im = jnp.where(reached, new_im, datum_im)
        for t in range(DATES):
            vre = v_ref[h, pl.ds(t * 8, STRIP)]
            vim = v_ref[h, pl.ds((16 + t) * 8, STRIP)]
            v_ref[h, pl.ds(t * 8, STRIP)] = vre * datum_re - vim * datum_im
            v_ref[h, pl.ds((16 + t) * 8, STRIP)] = vre * datum_im + vim * datum_re


def main_kernel(
    x_ref,
    halo_ref,
    map_ref,
    linked_ref,
    compressed_ref,
    plain,
    x2_ref,
    sums_ref,
    band_ref,
    scale_ref,
    g_ref,
    v_ref,
    c_ref,
    pick_ref,
    rows_ref,
    rows2_ref,
    send1,
    recv1,
    send2,
    recv2,
    spread_ref,
    sem_cs,
    sem_cr,
    sem_1s,
    sem_1r,
    sem_2s,
    sem_2r,
):
    section = lax.axis_index("stack")
    me = lax.axis_index("pix")
    y, rest = me // (NZ * NC), lax.rem(me, NZ * NC)
    z, c = rest // NC, lax.rem(rest, NC)
    g = y * NC + c

    sections = [lax.rem(section + o, SECT) for o in range(1, SECT)]
    group_of = [lax.rem(g + o, GROUPS) for o in range(1, GROUPS)]
    groups = [place(q // NC, z, lax.rem(q, NC)) for q in group_of]
    z_of = [lax.rem(z + o, NZ) for o in range(1, NZ)]
    depths = [place(y, q, c) for q in z_of]

    barrier = pltpu.get_barrier_semaphore()
    for peer in sections:
        pl.semaphore_signal(barrier, inc=1, device_id={"stack": peer}, device_id_type=MESH)
    for peer in groups + depths:
        pl.semaphore_signal(barrier, inc=1, device_id={"pix": peer}, device_id_type=MESH)

    m = iota((128, 128), 0)
    slot = (m >> 5) * 32 + (m & 15) * 2 + ((m >> 4) & 1)
    owner = jnp.broadcast_to(map_ref[...], (128, 128))
    chosen = one_hot(slot == owner)
    column = iota((128, 256), 1)
    block = iota((128, 256), 0)
    for k in range(2):
        pick = jnp.dot(chosen, one_hot(column == 2 * block + k), preferred_element_type=F32)
        pick_ref[:, k * 256 : (k + 1) * 256] = pick.astype(BF16)

    unpack(x_ref, plain, 0)
    unpack(halo_ref.at[0], plain, 1)
    unpack(halo_ref.at[1], plain, 2)
    for r in range(STRIP):
        spread(plain, 0, r, UP + r, x2_ref, None)
    for r in range(1, STRIP):
        spread(plain, 1, r, r - 1, x2_ref, me > 0)
    for r in range(UP):
        spread(plain, 2, r, UP + STRIP + r, x2_ref, me < BLOCKS - 1)
    coherences(x2_ref, sums_ref, band_ref, scale_ref, g_ref)
    power_iterations(g_ref, plain, v_ref, c_ref, section)

    pl.semaphore_wait(barrier, len(sections) + len(groups) + len(depths))

    sends = []

    def send(src, dst, ssem, rsem, device):
        copy = pltpu.make_async_remote_copy(
            src_ref=src, dst_ref=dst, send_sem=ssem, recv_sem=rsem,
            device_id=device, device_id_type=MESH,
        )
        copy.start()
        sends.append(copy)
        return copy

    first = [
        send(c_ref.at[section], c_ref.at[section], sem_cs.at[o], sem_cr.at[o], {"stack": peer})
        for o, peer in enumerate(sections)
    ]
    for copy in first:
        copy.wait_recv()
    connect(v_ref, c_ref, section)

    for h in range(2):
        lanes = slice(h * 128, (h + 1) * 128)
        for r in range(4):
            v = v_ref[h, pl.ds(r, FEAT, stride=8)].astype(BF16)
            rows_ref[r * FEAT : (r + 1) * FEAT, lanes] = v
        for r in range(2):
            v = v_ref[h, pl.ds(4 + r, FEAT, stride=8)].astype(BF16)
            for k in range(2):
                at = (k * 2 + r) * FEAT
                rows2_ref[at : at + FEAT, k * 256 + h * 128 : k * 256 + (h + 1) * 128] = v
                rows2_ref[at : at + FEAT, (1 - k) * 256 + h * 128 : (1 - k) * 256 + (h + 1) * 128] = (
                    jnp.zeros((FEAT, 128), BF16)
                )
    for k in range(2):
        part = lax.dot_general(
            pick_ref[:, k * 256 : (k + 1) * 256], rows_ref[...], NT_DIMS, preferred_element_type=F32
        ).astype(BF16)
        for q in range(GROUPS):
            send1[q, :, k * 128 : (k + 1) * 128] = part[q * 16 : (q + 1) * 16]
    part = lax.dot_general(
        pick_ref[...], rows2_ref[...], NT_DIMS, preferred_element_type=F32
    ).astype(BF16)
    for q in range(GROUPS):
        send1[q, :, 256:384] = part[q * 16 : (q + 1) * 16]

    second = [
        send(send1.at[q], recv1.at[g], sem_1s.at[o], sem_1r.at[o], {"pix": peer})
        for o, (q, peer) in enumerate(zip(group_of, groups))
    ]
    recv1[g] = send1[g]
    i, j = iota((128, 128), 0), iota((128, 128), 1)
    turn = one_hot(j == (i & 7) * 16 + (i >> 3))
    for copy in second:
        copy.wait_recv()
    got = recv1[...].reshape(128, 384)
    moved = jnp.dot(turn, got, preferred_element_type=F32)
    for q in range(NZ):
        send2[q] = moved[q * 8 : (q + 1) * 8].astype(BF16)
    order = sorted(range(NZ - 1), key=lambda o: -min(o + 1, NZ - 1 - o))
    third = [
        send(send2.at[z_of[o]], recv2.at[z], sem_2s.at[o], sem_2r.at[o], {"pix": depths[o]})
        for o in order
    ]
    recv2[z] = send2[z]
    n, lane = iota((128, ROWS), 0), iota((128, ROWS), 1)
    strip = ((n >> 1) & 3) * 32 + (n >> 3) * 2 + (n & 1)
    for r in range(STRIP):
        spread_ref[r * 128 : (r + 1) * 128] = one_hot(lane == strip * STRIP + r)
    for copy in third:
        copy.wait_recv()
    got = jnp.concatenate([recv2[q].astype(F32) for q in range(NZ)], axis=0)
    turned = got.T.astype(BF16)
    blocks = []
    for k in range(2):
        pieces = []
        for r in range(STRIP):
            at = k * 128 + r * FEAT if r < 4 else 256 + (k * 2 + r - 4) * FEAT
            pieces.append(turned[at : at + FEAT])
        blocks.append(jnp.concatenate(pieces, axis=1))
    out = jnp.dot(jnp.concatenate(blocks, axis=0), spread_ref[...], preferred_element_type=F32)
    for k in range(2):
        lanes = slice(k * ROWS, (k + 1) * ROWS)
        for part in range(2):
            at = k * FEAT + part * 16
            linked_ref[part, :, lanes] = out[at : at + DATES]
            compressed_ref[part : part + 1, lanes] = out[at + DATES : at + DATES + 1]
    for copy in sends:
        copy.wait_send()


def run_main(x, halo, owner_map):
    vmem = pl.BlockSpec(memory_space=pltpu.VMEM)
    return pl.pallas_call(
        main_kernel,
        out_shape=(
            jax.ShapeDtypeStruct((2, DATES, 2 * ROWS), F32),
            jax.ShapeDtypeStruct((2, 2 * ROWS), F32),
        ),
        in_specs=[vmem] * 3,
        out_specs=(vmem, vmem),
        scratch_shapes=[
            pltpu.VMEM((3, 2, DATES * STRIP * 2, 128), F32),
            pltpu.VMEM((2, 2, TALL * XS, 128), F32),
            pltpu.VMEM((8, STRIP * 32, 512), BF16),
            pltpu.VMEM((512, 256), BF16),
            pltpu.VMEM((2, STRIP * XS, 128), F32),
            pltpu.VMEM((2, 7 * 2 * 128, 128), F32),
            pltpu.VMEM((2, FEAT * 8, 128), F32),
            pltpu.VMEM((SECT, 2, 2, STRIP, 128), F32),
            pltpu.VMEM((128, 512), BF16),
            pltpu.VMEM((128, 256), BF16),
            pltpu.VMEM((128, 512), BF16),
            pltpu.VMEM((GROUPS, NZ, 384), BF16),
            pltpu.VMEM((GROUPS, NZ, 384), BF16),
            pltpu.VMEM((NZ, GROUPS, 384), BF16),
            pltpu.VMEM((NZ, GROUPS, 384), BF16),
            pltpu.VMEM((ROWS, ROWS), BF16),
            pltpu.SemaphoreType.DMA((SECT - 1,)),
            pltpu.SemaphoreType.DMA((SECT - 1,)),
            pltpu.SemaphoreType.DMA((GROUPS - 1,)),
            pltpu.SemaphoreType.DMA((GROUPS - 1,)),
            pltpu.SemaphoreType.DMA((NZ - 1,)),
            pltpu.SemaphoreType.DMA((NZ - 1,)),
        ],
        compiler_params=pltpu.CompilerParams(collective_id=1, has_side_effects=True),
        name="link",
    )(x, halo, owner_map)


def local(slc, owner_map):
    x = jnp.transpose(slc[:, 0], (1, 2, 0, 3))
    halo = exchange_halo(x)
    linked, compressed = run_main(x, halo, owner_map.reshape(1, BLOCKS))
    return (
        linked.reshape(2, 1, DATES, 1, 2 * ROWS),
        compressed.reshape(2, 1, 1, 2 * ROWS),
    )


def solution(mesh):
    in_specs = (P(None, "stack", None, "pix", None), P())
    out_specs = (P(None, "stack", None, "pix", None), P(None, "stack", "pix", None))
    return jax.shard_map(local, mesh=mesh, in_specs=in_specs, out_specs=out_specs, check_vma=False)
```

time: 212 us -> 45.2 us (0.21)
  the two profiles are of different devices: /device:TPU:6 before, /device:TPU:1 now
where the time goes in v1:
time: 45.2 us; the launch traced here: 45 us
  Pallas kernels  42 us (93%)
  local copies, waits for them, and re-layouts  2.41 us (5%)
  between operations  0.65 us (1%)
    pallas_call x1, Pallas kernels, run_main(): pl.pallas_call(main_kernel, out_shape=(jax.ShapeDtypeStruct((2, DATES, 2...  27.2 us
    pallas_call x1, Pallas kernels, exchange_halo(): pl.pallas_call(halo_kernel, out_shape=jax.ShapeDtypeStruct((2,) + x.shape...  14.8 us
    unnamed x4, local copies, waits for them, and re-layouts  2.41 us

profile of v1, /device:TPU:1, one launch (start us, length us, event | category | flops | bytes accessed | tf_op | source)
XLA Modules:
  0.0 45.0 jit_solution(11435938398914152071)
XLA Ops:
  0.6 14.8 %halo.1.halo_ref = bf16[2,15,6,2,256]{4,3,2,1,0:T(2,128)(2,1)} custom-call(bf16[15,6,2,256]{3,2,1,0:T(2,128)(2,1)} %bitcast.6), custom_call_target="tpu_custom_call" | custom-call | tf_op jit(solution)/shard_map/halo/pallas_call | solution.py:52
  15.4 27.2 %link.1 = (f32[2,15,1536]{2,1,0:T(8,128)}, f32[2,1536]{1,0:T(2,128)}) custom-call(bf16[15,6,2,256]{3,2,1,0:T(2,128)(2,1)} %bitcast.7, bf16[2,15,6,2,256]{4,3,2,1,0:T(2,128)(2,1)} %halo.1.halo_ref, s32[1,128]{1,0:T(1,128)} %bitcast.10), custom_call_target="tpu_custom_call" | custom-call | tf_op jit(solution)/shard_map/link/pallas_call | solution.py:436
  42.6 0.0 copy-start
  42.6 1.8 %copy.4 = f32[2,1,15,1,1536]{4,3,2,1,0:T(1,128)} copy(f32[2,1,15,1,1536]{4,2,0,3,1:T(8,128)} %bitcast.8) | data formatting | bytes 368640
  44.4 0.0 copy-done
  44.4 0.6 %copy.5 = f32[2,1,1,1536]{3,2,1,0:T(1,128)} copy(f32[2,1,1,1536]{3,0,2,1:T(2,128)S(1)} %bitcast.9) | data formatting | bytes 24576
Async XLA Ops:
  42.6 1.8 %copy-start = (f32[2,1536]{1,0:T(2,128)S(1)}, f32[2,1536]{1,0:T(2,128)}, u32[]{:S(2)}) copy-start(f32[2,1536]{1,0:T(2,128)} %get-tuple-element.5) | copy-start | bytes 36868

commit v2 on v1

v2 whole, which is shorter than its diff:
```python
import math

import jax
import jax.numpy as jnp
from jax import lax
from jax.experimental import pallas as pl
from jax.experimental.pallas import tpu as pltpu
from jax.sharding import PartitionSpec as P

MESH = pl.DeviceIdType.MESH
F32, BF16, I32 = jnp.float32, jnp.bfloat16, jnp.int32
DATES, ITERS, SECT, ROWS, COLS, BLOCKS = 15, 8, 4, 768, 256, 128
STRIP = 6
UP = 5
TALL = 16
NY, NZ, NC = 4, 16, 2
GROUPS = NY * NC
FEAT = 32
XS = 24
NT_DIMS = (((1,), (1,)), ((), ()))


def place(y, z, c):
    return y * (NZ * NC) + z * NC + c


def iota(shape, dim):
    return lax.broadcasted_iota(I32, shape, dim)


def one_hot(mask):
    return jnp.where(mask, 1.0, 0.0).astype(BF16)


def unpack(src_ref, plain, k, rows):
    for t in range(DATES):
        for r in range(rows):
            pair = src_ref[t, r].astype(F32)
            row = (t * STRIP + r) * 2
            plain[k, 0, pl.ds(row, 2)] = pair[:, :128]
            plain[k, 1, pl.ds(row, 2)] = pair[:, 128:]


def spread(plain, k, r, row, x_ref, keep):
    for h in range(2):
        for comp in range(2):
            v = plain[k, h, pl.ds(r * 2 + comp, DATES, stride=STRIP * 2)]
            if keep is not None:
                v = jnp.where(keep, v, 0.0)
            x_ref[comp, h, pl.ds(row * XS, DATES)] = v
            x_ref[comp, h, pl.ds(row * XS + DATES, 8)] = v[:8]


def add(x, y):
    return tuple(p + q for p, q in zip(x, y))


def middle_sum(terms):
    total = terms(UP)
    for row in range(UP + 1, UP + STRIP):
        total = add(total, terms(row))
    return total


def window_sums(terms, middle):
    total = middle
    sums = [None] * STRIP
    sums[5] = total
    for row in range(4, -1, -1):
        total = add(total, terms(row))
        sums[row] = total
    tail = None
    for r in range(1, STRIP):
        term = terms(r + 10)
        tail = term if tail is None else add(tail, term)
        sums[r] = add(sums[r], tail)
    return sums


def split_store(ref, lead, row, h, value):
    high = value.astype(BF16)
    low = (value - high.astype(F32)).astype(BF16)
    ref[lead, pl.ds(row, 16), h * 128 : (h + 1) * 128] = high
    ref[lead, pl.ds(row, 16), 256 + h * 128 : 256 + (h + 1) * 128] = low


def products(x_ref, h, d):
    def power(row):
        re = x_ref[0, h, pl.ds(row * XS, 16)]
        im = x_ref[1, h, pl.ds(row * XS, 16)]
        return (re * re + im * im,)

    def product(row):
        are = x_ref[0, h, pl.ds(row * XS, 16)]
        aim = x_ref[1, h, pl.ds(row * XS, 16)]
        bre = x_ref[0, h, pl.ds(row * XS + d, 16)]
        bim = x_ref[1, h, pl.ds(row * XS + d, 16)]
        return (are * bre + aim * bim, aim * bre - are * bim)

    return product if d else power


def middles(x_ref, mid_ref):
    for d in range(8):
        for h in range(2):
            for part, value in enumerate(middle_sum(products(x_ref, h, d))):
                mid_ref[d, h, part] = value


def coherences(x_ref, mid_ref, sums_ref, band_ref, scale_ref, g_ref):
    for d in range(8):
        parts = 2 if d else 1
        for h in range(2):
            middle = tuple(mid_ref[d, h, part] for part in range(parts))
            for r, value in enumerate(window_sums(products(x_ref, h, d), middle)):
                for part in range(parts):
                    split_store(sums_ref, d, (r * parts + part) * 16, h, value[part])
        rows = STRIP * parts * 16
        summed = jnp.dot(sums_ref[d, :rows], band_ref[...], preferred_element_type=F32)
        if not d:
            scale = lax.rsqrt(summed + 1.0)
            for h in range(2):
                for r in range(STRIP):
                    v = scale[r * 16 : (r + 1) * 16, h * 128 : (h + 1) * 128]
                    scale_ref[h, pl.ds(r * XS, 16)] = v
                    scale_ref[h, pl.ds(r * XS + DATES, 8)] = v[:8]
            continue
        for h in range(2):
            for r in range(STRIP):
                both = scale_ref[h, pl.ds(r * XS, 16)] * scale_ref[h, pl.ds(r * XS + d, 16)]
                row = r * 32
                re = summed[row : row + 16, h * 128 : (h + 1) * 128] * both
                im = summed[row + 16 : row + 32, h * 128 : (h + 1) * 128] * both
                re, im = re.astype(BF16).astype(F32), im.astype(BF16).astype(F32)
                base = (d - 1) * 384 + r
                g_ref[h, pl.ds(base, 16, stride=8)] = re
                g_ref[h, pl.ds(base + 128, 16, stride=8)] = re + im
                g_ref[h, pl.ds(base + 256, 16, stride=8)] = im - re


def power_iterations(g_ref, plain, v_ref, c_ref):
    def at(a, b):
        d = (b - a) % DATES
        flip = d > 7
        if flip:
            a, d = b, DATES - d
        return (d - 1) * 384 + a * 8, flip

    def normalized(parts):
        energy = None
        for re, im in parts:
            term = re * re + im * im
            energy = term if energy is None else energy + term
        factor = lax.rsqrt(energy * (1.0 / DATES) + 0.25)
        return tuple((re * factor, im * factor) for re, im in parts)

    def half(h, _):
        first = []
        for a in range(DATES):
            re, im = jnp.ones((STRIP, 128), F32), jnp.zeros((STRIP, 128), F32)
            for b in range(DATES):
                if b != a:
                    base, flip = at(a, b)
                    gre = g_ref[h, pl.ds(base, STRIP)]
                    gim = g_ref[h, pl.ds(base + 128, STRIP)] - gre
                    re = re + gre
                    im = im - gim if flip else im + gim
            first.append((re, im))
        vec = normalized(first)

        def step(_, vec):
            both = [re + im for re, im in vec]
            out = []
            for a in range(DATES):
                one, two, three = None, None, None
                for b in range(DATES):
                    if b != a:
                        base, flip = at(a, b)
                        vre, vim = vec[b]
                        gre = g_ref[h, pl.ds(base, STRIP)]
                        plus = g_ref[h, pl.ds(base + 128, STRIP)]
                        minus = g_ref[h, pl.ds(base + 256, STRIP)]
                        p1 = gre * both[b]
                        one = p1 if one is None else one + p1
                        p2, p3 = (plus * vre, minus * vim) if flip else (minus * vre, plus * vim)
                        if two is None:
                            two, three = (-p2, -p3) if flip else (p2, p3)
                        elif flip:
                            two, three = two - p2, three - p3
                        else:
                            two, three = two + p2, three + p3
                out.append((vec[a][0] + (one - three), vec[a][1] + (one + two)))
            return normalized(out)

        vec = lax.fori_loop(0, ITERS - 1, step, vec)
        packed_re, packed_im = None, None
        for t in range(DATES):
            vre, vim = vec[t]
            sre = plain[0, h, pl.ds(t * STRIP * 2, STRIP, stride=2)]
            sim = plain[0, h, pl.ds(t * STRIP * 2 + 1, STRIP, stride=2)]
            re = vre * sre + vim * sim
            im = vre * sim - vim * sre
            packed_re = re if packed_re is None else packed_re + re
            packed_im = im if packed_im is None else packed_im + im
            v_ref[h, pl.ds(t * 8, STRIP)] = vre
            v_ref[h, pl.ds((16 + t) * 8, STRIP)] = vim
        norm = 1.0 / math.sqrt(DATES)
        c_ref[0, h] = packed_re * norm
        c_ref[1, h] = packed_im * norm
        return 0

    lax.fori_loop(0, 2, half, 0)


def main_kernel(
    x_hbm,
    map_hbm,
    out_ref,
    map_ref,
    x_ref,
    halo_ref,
    plain,
    x2_ref,
    mid_ref,
    sums_ref,
    band_ref,
    scale_ref,
    g_ref,
    v_ref,
    c_ref,
    pick_ref,
    rows_ref,
    rows2_ref,
    rows3_ref,
    send1,
    recv1,
    sendc,
    recvc,
    send2,
    recv2,
    sem_x,
    sem_hs,
    sem_hr,
    sem_cs,
    sem_cr,
    sem_1s,
    sem_1r,
    sem_2s,
    sem_2r,
):
    section = lax.axis_index("stack")
    me = lax.axis_index("pix")
    y, rest = me // (NZ * NC), lax.rem(me, NZ * NC)
    z, c = rest // NC, lax.rem(rest, NC)
    g = y * NC + c

    sections = [lax.rem(section + o, SECT) for o in range(SECT)]
    group_of = [lax.rem(g + o, GROUPS) for o in range(GROUPS)]
    groups = [place(q // NC, z, lax.rem(q, NC)) for q in group_of]
    plane = [(s, o) for s in range(SECT) for o in range(GROUPS) if s or o]
    plane.sort(key=lambda so: -(min(so[0], 4 - so[0]) + min(so[1] // 2, 4 - so[1] // 2)))
    z_of = [lax.rem(z + o, NZ) for o in range(1, NZ)]
    depths = [place(y, q, c) for q in z_of]
    after, before = lax.rem(me + 1, BLOCKS), lax.rem(me + BLOCKS - 1, BLOCKS)
    other = lax.rem(me + BLOCKS + 2 * c - 1, BLOCKS)

    def device(s, o):
        return {"stack": sections[s], "pix": groups[o]}

    barrier = pltpu.get_barrier_semaphore()
    pl.semaphore_signal(barrier, inc=1, device_id={"pix": other}, device_id_type=MESH)
    for s, o in reversed(plane):
        pl.semaphore_signal(barrier, inc=1, device_id=device(s, o), device_id_type=MESH)
    for peer in depths:
        pl.semaphore_signal(barrier, inc=1, device_id={"pix": peer}, device_id_type=MESH)
    slots = pltpu.make_async_copy(map_hbm, map_ref, sem_x.at[0])
    slots.start()
    own = pltpu.make_async_copy(x_hbm, x_ref, sem_x.at[1])
    own.start()
    pl.semaphore_wait(barrier, 1 + len(plane) + len(depths))

    sends = []

    def send(src, dst, ssem, rsem, device):
        copy = pltpu.make_async_remote_copy(
            src_ref=src, dst_ref=dst, send_sem=ssem, recv_sem=rsem,
            device_id=device, device_id_type=MESH,
        )
        copy.start()
        sends.append(copy)
        return copy

    halos = [
        send(x_hbm.at[:, 1:6], halo_ref.at[0], sem_hs.at[0], sem_hr.at[0], {"pix": after}),
        send(x_hbm.at[:, 0:5], halo_ref.at[1], sem_hs.at[1], sem_hr.at[1], {"pix": before}),
    ]

    m = iota((128, 128), 0)
    slot = (m >> 5) * 32 + (m & 15) * 2 + ((m >> 4) & 1)
    slots.wait()
    owner = jnp.broadcast_to(map_ref[...], (128, 128))
    chosen = one_hot(slot == owner)
    column = iota((128, 256), 1)
    block = iota((128, 256), 0)
    for k in range(2):
        pick = jnp.dot(chosen, one_hot(column == 2 * block + k), preferred_element_type=F32)
        pick_ref[:, k * 256 : (k + 1) * 256] = pick.astype(BF16)
    band_ref[...] = one_hot(
        jnp.abs((iota((512, 256), 0) & 255) - iota((512, 256), 1)) <= 2
    )
    rows3_ref[...] = jnp.zeros((128, 512), F32)
    for h in range(2):
        for part in range(2):
            v_ref[h, pl.ds((part * 16 + DATES) * 8, 8)] = jnp.zeros((8, 128), F32)

    own.wait()
    unpack(x_ref, plain, 0, STRIP)
    for r in range(STRIP):
        spread(plain, 0, r, UP + r, x2_ref, None)
    middles(x2_ref, mid_ref)
    for copy in halos:
        copy.wait_recv()
    unpack(halo_ref.at[0], plain, 1, UP)
    unpack(halo_ref.at[1], plain, 2, UP)
    for r in range(UP):
        spread(plain, 1, r, r, x2_ref, me > 0)
        spread(plain, 2, r, UP + STRIP + r, x2_ref, me < BLOCKS - 1)
    coherences(x2_ref, mid_ref, sums_ref, band_ref, scale_ref, g_ref)
    power_iterations(g_ref, plain, v_ref, c_ref)

    for h in range(2):
        for comp in range(2):
            for k in range(2):
                at = pl.multiple_of(comp * 64 + k * 32 + section * 8, 8)
                lanes = slice(k * 256 + h * 128, k * 256 + (h + 1) * 128)
                rows3_ref[pl.ds(at, STRIP), lanes] = c_ref[comp, h]
    part = lax.dot_general(
        pick_ref[...], rows3_ref[...].astype(BF16), NT_DIMS, preferred_element_type=F32
    ).astype(BF16)
    for q in range(GROUPS):
        sendc[q] = part[q * 16 : (q + 1) * 16]
    first = [
        send(sendc.at[group_of[o]], recvc.at[section, g], sem_cs.at[s, o], sem_cr.at[s, o], device(s, o))
        for s, o in plane
    ]

    for h in range(2):
        lanes = slice(h * 128, (h + 1) * 128)
        for r in range(4):
            v = v_ref[h, pl.ds(r, FEAT, stride=8)].astype(BF16)
            rows_ref[r * FEAT : (r + 1) * FEAT, lanes] = v
        for r in range(2):
            v = v_ref[h, pl.ds(4 + r, FEAT, stride=8)].astype(BF16)
            for k in range(2):
                at = (k * 2 + r) * FEAT
                rows2_ref[at : at + FEAT, k * 256 + h * 128 : k * 256 + (h + 1) * 128] = v
                rows2_ref[at : at + FEAT, (1 - k) * 256 + h * 128 : (1 - k) * 256 + (h + 1) * 128] = (
                    jnp.zeros((FEAT, 128), BF16)
                )
    for k in range(2):
        part = lax.dot_general(
            pick_ref[:, k * 256 : (k + 1) * 256], rows_ref[...], NT_DIMS, preferred_element_type=F32
        ).astype(BF16)
        for q in range(GROUPS):
            send1[q, :, k * 128 : (k + 1) * 128] = part[q * 16 : (q + 1) * 16]
    part = lax.dot_general(
        pick_ref[...], rows2_ref[...], NT_DIMS, preferred_element_type=F32
    ).astype(BF16)
    for q in range(GROUPS):
        send1[q, :, 256:384] = part[q * 16 : (q + 1) * 16]
    second = [
        send(send1.at[group_of[o]], recv1.at[g], sem_1s.at[o], sem_1r.at[o], device(0, o))
        for s, o in plane
        if s == 0
    ]
    recvc[section, g] = sendc[g]
    recv1[g] = send1[g]
    i, j = iota((128, 128), 0), iota((128, 128), 1)
    turn = one_hot(j == (i & 7) * 16 + (i >> 3))
    for copy in first + second:
        copy.wait_recv()
    got = recv1[...].reshape(128, 384)
    moved = jnp.dot(turn, got, preferred_element_type=F32)
    for q in range(NZ):
        send2[q, :, :384] = moved[q * 8 : (q + 1) * 8].astype(BF16)
    packed = (recvc[0] + recvc[1] + recvc[2] + recvc[3]).reshape(128, 128)
    moved = jnp.dot(turn, packed, preferred_element_type=F32)
    for q in range(NZ):
        send2[q, :, 384:] = moved[q * 8 : (q + 1) * 8].astype(BF16)
    order = sorted(range(NZ - 1), key=lambda o: -min(o + 1, NZ - 1 - o))
    third = [
        send(send2.at[z_of[o]], recv2.at[z], sem_2s.at[o], sem_2r.at[o], {"pix": depths[o]})
        for o in order
    ]
    recv2[z] = send2[z]
    for copy in third:
        copy.wait_recv()
    out_ref[...] = recv2[...]
    for copy in sends:
        copy.wait_send()


def run_main(x, owner_map):
    vmem = pl.BlockSpec(memory_space=pltpu.VMEM)
    dma = pltpu.SemaphoreType.DMA
    return pl.pallas_call(
        main_kernel,
        out_shape=jax.ShapeDtypeStruct((NZ, GROUPS, 512), BF16),
        in_specs=[pl.BlockSpec(memory_space=pltpu.HBM)] * 2,
        out_specs=vmem,
        scratch_shapes=[
            pltpu.VMEM((1, BLOCKS), I32),
            pltpu.VMEM((DATES, STRIP, 2, COLS), BF16),
            pltpu.VMEM((2, DATES, UP, 2, COLS), BF16),
            pltpu.VMEM((3, 2, DATES * STRIP * 2, 128), F32),
            pltpu.VMEM((2, 2, TALL * XS, 128), F32),
            pltpu.VMEM((8, 2, 2, 16, 128), F32),
            pltpu.VMEM((8, STRIP * 32, 512), BF16),
            pltpu.VMEM((512, 256), BF16),
            pltpu.VMEM((2, STRIP * XS, 128), F32),
            pltpu.VMEM((2, 7 * 3 * 128, 128), F32),
            pltpu.VMEM((2, FEAT * 8, 128), F32),
            pltpu.VMEM((2, 2, STRIP, 128), F32),
            pltpu.VMEM((128, 512), BF16),
            pltpu.VMEM((128, 256), BF16),
            pltpu.VMEM((128, 512), BF16),
            pltpu.VMEM((128, 512), F32),
            pltpu.VMEM((GROUPS, NZ, 384), BF16),
            pltpu.VMEM((GROUPS, NZ, 384), BF16),
            pltpu.VMEM((GROUPS, NZ, 128), BF16),
            pltpu.VMEM((SECT, GROUPS, NZ, 128), BF16),
            pltpu.VMEM((NZ, GROUPS, 512), BF16),
            pltpu.VMEM((NZ, GROUPS, 512), BF16),
            dma((2,)),
            dma((2,)),
            dma((2,)),
            dma((SECT, GROUPS)),
            dma((SECT, GROUPS)),
            dma((GROUPS,)),
            dma((GROUPS,)),
            dma((NZ - 1,)),
            dma((NZ - 1,)),
        ],
        compiler_params=pltpu.CompilerParams(
            collective_id=0, has_side_effects=True, vmem_limit_bytes=20 * 1024 * 1024
        ),
        name="link",
    )(x, owner_map)


def finish_kernel(got_ref, linked_ref, compressed_ref, turned_ref, spread_ref):
    section = lax.axis_index("stack")
    n, lane = iota((128, ROWS), 0), iota((128, ROWS), 1)
    strip = ((n >> 1) & 3) * 32 + (n >> 3) * 2 + (n & 1)
    for r in range(STRIP):
        spread_ref[r * 128 : (r + 1) * 128] = one_hot(lane == strip * STRIP + r)
    got = jnp.concatenate([got_ref[q].astype(F32) for q in range(NZ)], axis=0)
    for tile in range(4):
        turned_ref[tile * 128 : (tile + 1) * 128] = got[:, tile * 128 : (tile + 1) * 128].T
    blocks = []
    for k in range(2):
        pieces = []
        for r in range(STRIP):
            at = k * 128 + r * FEAT if r < 4 else 256 + (k * 2 + r - 4) * FEAT
            pieces.append(turned_ref[pl.ds(at, FEAT)].astype(BF16))
        blocks.append(jnp.concatenate(pieces, axis=1))
    pieces = []
    for r in range(STRIP):
        pair = [turned_ref[pl.ds(384 + comp * 64 + r, 8, stride=8)] for comp in range(2)]
        pieces.append(jnp.concatenate(pair, axis=0).astype(BF16))
    blocks.append(jnp.concatenate(pieces, axis=1))
    out = jnp.dot(jnp.concatenate(blocks, axis=0), spread_ref[...], preferred_element_type=F32)
    re, im = out[64:72], out[72:80]
    link_re = re[1:] * re[:-1] + im[1:] * im[:-1]
    link_im = im[1:] * re[:-1] - re[1:] * im[:-1]
    factor = lax.rsqrt(link_re * link_re + link_im * link_im + 1.0)
    unit_re, unit_im = link_re * factor, link_im * factor
    tiles = ROWS // 128
    for k in range(2):
        datum_re, datum_im = jnp.ones((1, ROWS), F32), jnp.zeros((1, ROWS), F32)
        mine_re, mine_im = re[k * 4 : k * 4 + 1], im[k * 4 : k * 4 + 1]
        for j in range(SECT - 1):
            at = k * 4 + j
            ure, uim = unit_re[at : at + 1], unit_im[at : at + 1]
            new_re = datum_re * ure - datum_im * uim
            new_im = datum_re * uim + datum_im * ure
            reached = j < section
            datum_re = jnp.where(reached, new_re, datum_re)
            datum_im = jnp.where(reached, new_im, datum_im)
            mine_re = jnp.where(reached, re[at + 1 : at + 2], mine_re)
            mine_im = jnp.where(reached, im[at + 1 : at + 2], mine_im)
        at = k * FEAT
        vre, vim = out[at : at + DATES], out[at + 16 : at + 16 + DATES]
        linked = (vre * datum_re - vim * datum_im, vre * datum_im + vim * datum_re)
        mine = (mine_re, mine_im)
        for part in range(2):
            for tile in range(tiles):
                row = part * DATES * 2 * tiles + k * tiles + tile
                lanes = slice(tile * 128, (tile + 1) * 128)
                linked_ref[pl.ds(row, DATES, stride=2 * tiles)] = linked[part][:, lanes]
                row = part * 2 * tiles + k * tiles + tile
                compressed_ref[pl.ds(row, 1)] = mine[part][:, lanes]


def run_finish(got):
    vmem = pl.BlockSpec(memory_space=pltpu.VMEM)
    return pl.pallas_call(
        finish_kernel,
        out_shape=(
            jax.ShapeDtypeStruct((2 * DATES * 12, 128), F32),
            jax.ShapeDtypeStruct((24, 128), F32),
        ),
        in_specs=[vmem],
        out_specs=(vmem, vmem),
        scratch_shapes=[pltpu.VMEM((512, 128), F32), pltpu.VMEM((ROWS, ROWS), BF16)],
        compiler_params=pltpu.CompilerParams(vmem_limit_bytes=20 * 1024 * 1024),
        name="finish",
    )(got)


def local(slc, owner_map):
    x = jnp.transpose(slc[:, 0], (1, 2, 0, 3))
    linked, compressed = run_finish(run_main(x, owner_map.reshape(1, BLOCKS)))
    return (
        linked.reshape(2, 1, DATES, 1, 2 * ROWS),
        compressed.reshape(2, 1, 1, 2 * ROWS),
    )


def solution(mesh):
    in_specs = (P(None, "stack", None, "pix", None), P())
    out_specs = (P(None, "stack", None, "pix", None), P(None, "stack", "pix", None))
    return jax.shard_map(local, mesh=mesh, in_specs=in_specs, out_specs=out_specs, check_vma=False)
```

time: 45.2 us -> 44.7 us (0.989)
  local copies, waits for them, and re-layouts: 2.41 us -> 1.54 us
    unnamed x4, local copies, waits for them, and re-layouts: 2.41 us -> 1.54 us
where the time goes in v2:
time: 44.7 us; the launch traced here: 44.6 us
  Pallas kernels  42.4 us (95%)
  local copies, waits for them, and re-layouts  1.54 us (3%)
  between operations  0.65 us (1%)
    pallas_call x1, Pallas kernels, run_main(): pl.pallas_call(main_kernel, out_shape=jax.ShapeDtypeStruct((NZ, GROUPS, 5...  41.3 us
    unnamed x4, local copies, waits for them, and re-layouts  1.54 us
    pallas_call x1, Pallas kernels, run_finish(): pl.pallas_call(finish_kernel, out_shape=(jax.ShapeDtypeStruct((2 * DATES...  1.09 us

profile of v2, /device:TPU:1, one launch (start us, length us, event | category | flops | bytes accessed | tf_op | source)
XLA Modules:
  0.0 44.6 jit_solution(18314318668743096276)
XLA Ops:
  0.6 0.0 copy-start.1
  0.6 0.6 %copy-done.1 = s32[128]{0:T(128)S(1)} copy-done((s32[128]{0:T(128)S(1)}, s32[128]{0:T(128)}, u32[]{:S(2)}) %copy-start.1) | copy-done | bytes 536
  1.3 0.0 copy-start
  1.3 0.9 %copy-done = bf16[2,1,15,6,256]{4,0,3,2,1:T(2,128)(2,1)S(1)} copy-done((bf16[2,1,15,6,256]{4,0,3,2,1:T(2,128)(2,1)S(1)}, bf16[2,1,15,6,256]{4,0,3,2,1:T(2,128)(2,1)}, u32[]{:S(2)}) %copy-start) | copy-done | bytes 92184
  2.2 41.3 %link.1.got_ref = bf16[16,8,512]{2,1,0:T(8,128)(2,1)S(1)} custom-call(bf16[15,6,2,256]{3,2,1,0:T(2,128)(2,1)S(1)} %bitcast.6, s32[1,128]{1,0:T(1,128)S(1)} %bitcast.7), custom_call_target="tpu_custom_call" | custom-call | tf_op jit(solution)/shard_map/link/pallas_call | solution.py:406
  43.5 1.1 %finish.1 = (f32[360,128]{1,0:T(8,128)}, f32[24,128]{1,0:T(8,128)}) custom-call(bf16[16,8,512]{2,1,0:T(8,128)(2,1)S(1)} %link.1.got_ref), custom_call_target="tpu_custom_call" | custom-call | tf_op jit(solution)/shard_map/finish/pallas_call | solution.py:507
Async XLA Ops:
  0.6 0.7 %copy-start.1 = (s32[128]{0:T(128)S(1)}, s32[128]{0:T(128)}, u32[]{:S(2)}) copy-start(s32[128]{0:T(128)} %param.3) | copy-start | bytes 1540
  1.3 0.9 %copy-start = (bf16[2,1,15,6,256]{4,0,3,2,1:T(2,128)(2,1)S(1)}, bf16[2,1,15,6,256]{4,0,3,2,1:T(2,128)(2,1)}, u32[]{:S(2)}) copy-start(bf16[2,1,15,6,256]{4,0,3,2,1:T(2,128)(2,1)} %param.2) | copy-start | bytes 276484

commit v3 on v2

--- a/solution.py
+++ b/solution.py
@@ -238,6 +238,7 @@
     recvc,
     send2,
     recv2,
+    sem_t,
     sem_x,
     sem_hs,
     sem_hr,
@@ -267,17 +268,32 @@
     def device(s, o):
         return {"stack": sections[s], "pix": groups[o]}
 
+    def at_x(o):
+        return {"stack": lax.rem(section + o, SECT)}
+
+    def at_y(o):
+        return {"pix": place(lax.rem(y + o, NY), z, c)}
+
+    def at_z(o):
+        return {"pix": place(y, lax.rem(z + o, NZ), c)}
+
+    at_core = {"pix": place(y, z, 1 - c)}
+    nearest = [
+        {"pix": other}, at_core, at_z(1), at_z(NZ - 1), at_y(1), at_y(NY - 1), at_x(1), at_x(SECT - 1)
+    ]
     barrier = pltpu.get_barrier_semaphore()
-    pl.semaphore_signal(barrier, inc=1, device_id={"pix": other}, device_id_type=MESH)
-    for s, o in reversed(plane):
-        pl.semaphore_signal(barrier, inc=1, device_id=device(s, o), device_id_type=MESH)
-    for peer in depths:
-        pl.semaphore_signal(barrier, inc=1, device_id={"pix": peer}, device_id_type=MESH)
+    for peer in nearest:
+        pl.semaphore_signal(barrier, inc=1, device_id=peer, device_id_type=MESH)
+
+    def tell(sem, peers):
+        for peer in peers:
+            pl.semaphore_signal(sem, inc=1, device_id=peer, device_id_type=MESH)
+
     slots = pltpu.make_async_copy(map_hbm, map_ref, sem_x.at[0])
     slots.start()
     own = pltpu.make_async_copy(x_hbm, x_ref, sem_x.at[1])
     own.start()
-    pl.semaphore_wait(barrier, 1 + len(plane) + len(depths))
+    pl.semaphore_wait(barrier, len(nearest))
 
     sends = []
 
@@ -294,6 +310,10 @@
         send(x_hbm.at[:, 1:6], halo_ref.at[0], sem_hs.at[0], sem_hr.at[0], {"pix": after}),
         send(x_hbm.at[:, 0:5], halo_ref.at[1], sem_hs.at[1], sem_hr.at[1], {"pix": before}),
     ]
+
+    tell(sem_t.at[0], [at_x(1)])
+    tell(sem_t.at[1], [at_y(1)])
+    tell(sem_t.at[2], [at_z(1), at_z(NZ - 1)])
 
     m = iota((128, 128), 0)
     slot = (m >> 5) * 32 + (m & 15) * 2 + ((m >> 4) & 1)
@@ -318,6 +338,11 @@
     for r in range(STRIP):
         spread(plain, 0, r, UP + r, x2_ref, None)
     middles(x2_ref, mid_ref)
+    pl.semaphore_wait(sem_t.at[0], 1)
+    pl.semaphore_wait(sem_t.at[1], 1)
+    pl.semaphore_wait(sem_t.at[2], 2)
+    tell(sem_t.at[3], [at_y(1), at_y(2), at_y(3)])
+    tell(sem_t.at[4], [at_z(2), at_z(NZ - 2)])
     for copy in halos:
         copy.wait_recv()
     unpack(halo_ref.at[0], plain, 1, UP)
@@ -326,7 +351,13 @@
         spread(plain, 1, r, r, x2_ref, me > 0)
         spread(plain, 2, r, UP + STRIP + r, x2_ref, me < BLOCKS - 1)
     coherences(x2_ref, mid_ref, sums_ref, band_ref, scale_ref, g_ref)
+    pl.semaphore_wait(sem_t.at[3], 3)
+    pl.semaphore_wait(sem_t.at[4], 2)
+    tell(sem_t.at[5], [at_core])
+    tell(sem_t.at[6], [at_z(4), at_z(NZ - 4)])
     power_iterations(g_ref, plain, v_ref, c_ref)
+    pl.semaphore_wait(sem_t.at[5], 1)
+    pl.semaphore_wait(sem_t.at[6], 2)
 
     for h in range(2):
         for comp in range(2):
@@ -431,6 +462,7 @@
             pltpu.VMEM((SECT, GROUPS, NZ, 128), BF16),
             pltpu.VMEM((NZ, GROUPS, 512), BF16),
             pltpu.VMEM((NZ, GROUPS, 512), BF16),
+            pltpu.SemaphoreType.REGULAR((7,)),
             dma((2,)),
             dma((2,)),
             dma((2,)),
@@ -520,7 +552,7 @@
 
 def local(slc, owner_map):
     x = jnp.transpose(slc[:, 0], (1, 2, 0, 3))
-    linked, compressed = run_finish(run_main(x, owner_map.reshape(1, BLOCKS)))
+    linked, compressed = run_finish(run_main(pltpu.with_memory_space_constraint(x, pltpu.HBM), pltpu.with_memory_space_constraint(owner_map.reshape(1, BLOCKS), pltpu.HBM)))
     return (
         linked.reshape(2, 1, DATES, 1, 2 * ROWS),
         compressed.reshape(2, 1, 1, 2 * ROWS),

time: 44.7 us -> 39.8 us (0.89)
  the two profiles are of different devices: /device:TPU:1 before, /device:TPU:6 now
where the time goes in v3:
time: 39.8 us; the launch traced here: 39 us
  Pallas kernels  38.4 us (96%)
  between operations  0.64 us (2%)
    pallas_call x1, Pallas kernels, run_main(): pl.pallas_call(main_kernel, out_shape=jax.ShapeDtypeStruct((NZ, GROUPS, 5...  37.3 us
    pallas_call x1, Pallas kernels, run_finish(): pl.pallas_call(finish_kernel, out_shape=(jax.ShapeDtypeStruct((2 * DATES...  1.09 us

profile of v3, /device:TPU:6, one launch (start us, length us, event | category | flops | bytes accessed | tf_op | source)
XLA Modules:
  0.0 39.0 jit_solution(13154527523148799625)
XLA Ops:
  0.6 37.3 %link.1.got_ref = bf16[16,8,512]{2,1,0:T(8,128)(2,1)S(1)} custom-call(bf16[15,6,2,256]{3,2,1,0:T(2,128)(2,1)} %bitcast.6, s32[1,128]{1,0:T(1,128)} %bitcast.7), custom_call_target="tpu_custom_call" | custom-call | tf_op jit(solution)/shard_map/link/pallas_call | solution.py:437
  37.9 1.1 %finish.1 = (f32[360,128]{1,0:T(8,128)}, f32[24,128]{1,0:T(8,128)}) custom-call(bf16[16,8,512]{2,1,0:T(8,128)(2,1)S(1)} %link.1.got_ref), custom_call_target="tpu_custom_call" | custom-call | tf_op jit(solution)/shard_map/finish/pallas_call | solution.py:539

commit v4 on v3

--- a/solution.py
+++ b/solution.py
@@ -146,13 +146,15 @@
             a, d = b, DATES - d
         return (d - 1) * 384 + a * 8, flip
 
-    def normalized(parts):
-        energy = None
+    def energy(parts):
+        total = None
         for re, im in parts:
             term = re * re + im * im
-            energy = term if energy is None else energy + term
-        factor = lax.rsqrt(energy * (1.0 / DATES) + 0.25)
-        return tuple((re * factor, im * factor) for re, im in parts)
+            total = term if total is None else total + term
+        return total
+
+    def rescaled(scale, parts):
+        return scale * lax.rsqrt(scale * scale * energy(parts) * (1.0 / DATES) + 0.25)
 
     def half(h, _):
         first = []
@@ -166,33 +168,35 @@
                     re = re + gre
                     im = im - gim if flip else im + gim
             first.append((re, im))
-        vec = normalized(first)
-
-        def step(_, vec):
+
+        def step(_, carry):
+            vec, scale = carry
+            scale = rescaled(scale, vec)
             both = [re + im for re, im in vec]
+            def matvec(a, first, second, ops):
+                total = None
+                for step in range(1, DATES):
+                    b = (a + step) % DATES
+                    base, flip = at(a, b)
+                    term = g_ref[h, pl.ds(base + (second if flip else first), STRIP)] * ops[b]
+                    if total is None:
+                        total = term
+                    else:
+                        total = total - term if flip and first else total + term
+                return total
+
+            ones = [matvec(a, 0, 0, both) for a in range(DATES)]
+            twos = [ones[a] + matvec(a, 256, 128, [v[0] for v in vec]) for a in range(DATES)]
             out = []
             for a in range(DATES):
-                one, two, three = None, None, None
-                for b in range(DATES):
-                    if b != a:
-                        base, flip = at(a, b)
-                        vre, vim = vec[b]
-                        gre = g_ref[h, pl.ds(base, STRIP)]
-                        plus = g_ref[h, pl.ds(base + 128, STRIP)]
-                        minus = g_ref[h, pl.ds(base + 256, STRIP)]
-                        p1 = gre * both[b]
-                        one = p1 if one is None else one + p1
-                        p2, p3 = (plus * vre, minus * vim) if flip else (minus * vre, plus * vim)
-                        if two is None:
-                            two, three = (-p2, -p3) if flip else (p2, p3)
-                        elif flip:
-                            two, three = two - p2, three - p3
-                        else:
-                            two, three = two + p2, three + p3
-                out.append((vec[a][0] + (one - three), vec[a][1] + (one + two)))
-            return normalized(out)
-
-        vec = lax.fori_loop(0, ITERS - 1, step, vec)
+                three = matvec(a, 128, 256, [v[1] for v in vec])
+                out.append((vec[a][0] + (ones[a] - three), vec[a][1] + twos[a]))
+            return tuple(out), scale
+
+        carry = (tuple(first), jnp.ones((STRIP, 128), F32))
+        vec, scale = lax.fori_loop(0, ITERS - 1, step, carry, unroll=True)
+        scale = rescaled(scale, vec)
+        vec = [(re * scale, im * scale) for re, im in vec]
         packed_re, packed_im = None, None
         for t in range(DATES):
             vre, vim = vec[t]
@@ -216,6 +220,7 @@
     x_hbm,
     map_hbm,
     out_ref,
+    spread_ref,
     map_ref,
     x_ref,
     halo_ref,
@@ -251,22 +256,9 @@
 ):
     section = lax.axis_index("stack")
     me = lax.axis_index("pix")
-    y, rest = me // (NZ * NC), lax.rem(me, NZ * NC)
-    z, c = rest // NC, lax.rem(rest, NC)
-    g = y * NC + c
-
-    sections = [lax.rem(section + o, SECT) for o in range(SECT)]
-    group_of = [lax.rem(g + o, GROUPS) for o in range(GROUPS)]
-    groups = [place(q // NC, z, lax.rem(q, NC)) for q in group_of]
-    plane = [(s, o) for s in range(SECT) for o in range(GROUPS) if s or o]
-    plane.sort(key=lambda so: -(min(so[0], 4 - so[0]) + min(so[1] // 2, 4 - so[1] // 2)))
-    z_of = [lax.rem(z + o, NZ) for o in range(1, NZ)]
-    depths = [place(y, q, c) for q in z_of]
-    after, before = lax.rem(me + 1, BLOCKS), lax.rem(me + BLOCKS - 1, BLOCKS)
+    y, rest = lax.div(me, NZ * NC), lax.rem(me, NZ * NC)
+    z, c = lax.div(rest, NC), lax.rem(rest, NC)
     other = lax.rem(me + BLOCKS + 2 * c - 1, BLOCKS)
-
-    def device(s, o):
-        return {"stack": sections[s], "pix": groups[o]}
 
     def at_x(o):
         return {"stack": lax.rem(section + o, SECT)}
@@ -306,6 +298,7 @@
         sends.append(copy)
         return copy
 
+    after, before = lax.rem(me + 1, BLOCKS), lax.rem(me + BLOCKS - 1, BLOCKS)
     halos = [
         send(x_hbm.at[:, 1:6], halo_ref.at[0], sem_hs.at[0], sem_hr.at[0], {"pix": after}),
         send(x_hbm.at[:, 0:5], halo_ref.at[1], sem_hs.at[1], sem_hr.at[1], {"pix": before}),
@@ -314,6 +307,13 @@
     tell(sem_t.at[0], [at_x(1)])
     tell(sem_t.at[1], [at_y(1)])
     tell(sem_t.at[2], [at_z(1), at_z(NZ - 1)])
+
+    g = y * NC + c
+    group_of = [lax.rem(g + o, GROUPS) for o in range(GROUPS)]
+    groups = [place(lax.div(q, NC), z, lax.rem(q, NC)) for q in group_of]
+    far = sorted(range(GROUPS), key=lambda o: -min(o // 2, 4 - o // 2))
+    z_of = [lax.rem(z + o, NZ) for o in range(1, NZ)]
+    depths = [place(y, q, c) for q in z_of]
 
     m = iota((128, 128), 0)
     slot = (m >> 5) * 32 + (m & 15) * 2 + ((m >> 4) & 1)
@@ -370,9 +370,24 @@
     ).astype(BF16)
     for q in range(GROUPS):
         sendc[q] = part[q * 16 : (q + 1) * 16]
-    first = [
-        send(sendc.at[group_of[o]], recvc.at[section, g], sem_cs.at[s, o], sem_cr.at[s, o], device(s, o))
-        for s, o in plane
+    def later(s, o):
+        return pltpu.make_async_remote_copy(
+            src_ref=sendc.at[group_of[o]], dst_ref=recvc.at[section, g],
+            send_sem=sem_cs.at[s, o], recv_sem=sem_cr.at[s, o],
+            device_id={"stack": section + s, "pix": groups[o]}, device_id_type=MESH,
+        )
+
+    for s in (2, 3, 1):
+
+        @pl.when(section + s < SECT)
+        def _():
+            for o in far:
+                later(s, o).start()
+
+    here = [
+        send(sendc.at[group_of[o]], recvc.at[section, g], sem_cs.at[0, o], sem_cr.at[0, o], {"pix": groups[o]})
+        for o in far
+        if o
     ]
 
     for h in range(2):
@@ -399,22 +414,32 @@
     ).astype(BF16)
     for q in range(GROUPS):
         send1[q, :, 256:384] = part[q * 16 : (q + 1) * 16]
-    second = [
-        send(send1.at[group_of[o]], recv1.at[g], sem_1s.at[o], sem_1r.at[o], device(0, o))
-        for s, o in plane
-        if s == 0
+    here += [
+        send(send1.at[group_of[o]], recv1.at[g], sem_1s.at[o], sem_1r.at[o], {"pix": groups[o]})
+        for o in far
+        if o
     ]
     recvc[section, g] = sendc[g]
     recv1[g] = send1[g]
     i, j = iota((128, 128), 0), iota((128, 128), 1)
     turn = one_hot(j == (i & 7) * 16 + (i >> 3))
-    for copy in first + second:
+    for copy in here:
         copy.wait_recv()
+    for s in range(1, SECT):
+
+        @pl.when(section >= s)
+        def _():
+            for o in range(GROUPS):
+                later(s, o).wait_recv()
+
     got = recv1[...].reshape(128, 384)
     moved = jnp.dot(turn, got, preferred_element_type=F32)
     for q in range(NZ):
         send2[q, :, :384] = moved[q * 8 : (q + 1) * 8].astype(BF16)
-    packed = (recvc[0] + recvc[1] + recvc[2] + recvc[3]).reshape(128, 128)
+    packed = recvc[0]
+    for s in range(1, SECT):
+        packed = jnp.where(section >= s, packed + recvc[s], packed)
+    packed = packed.reshape(128, 128)
     moved = jnp.dot(turn, packed, preferred_element_type=F32)
     for q in range(NZ):
         send2[q, :, 384:] = moved[q * 8 : (q + 1) * 8].astype(BF16)
@@ -424,11 +449,21 @@
         for o in order
     ]
     recv2[z] = send2[z]
+    n, lane = iota((128, ROWS), 0), iota((128, ROWS), 1)
+    strip = ((n >> 1) & 3) * 32 + (n >> 3) * 2 + (n & 1)
+    for r in range(STRIP):
+        spread_ref[r * 128 : (r + 1) * 128] = one_hot(lane == strip * STRIP + r)
     for copy in third:
         copy.wait_recv()
     out_ref[...] = recv2[...]
     for copy in sends:
         copy.wait_send()
+    for s in range(1, SECT):
+
+        @pl.when(section + s < SECT)
+        def _():
+            for o in range(GROUPS):
+                later(s, o).wait_send()
 
 
 def run_main(x, owner_map):
@@ -436,9 +471,12 @@
     dma = pltpu.SemaphoreType.DMA
     return pl.pallas_call(
         main_kernel,
-        out_shape=jax.ShapeDtypeStruct((NZ, GROUPS, 512), BF16),
+        out_shape=(
+            jax.ShapeDtypeStruct((NZ, GROUPS, 512), BF16),
+            jax.ShapeDtypeStruct((ROWS, ROWS), BF16),
+        ),
         in_specs=[pl.BlockSpec(memory_space=pltpu.HBM)] * 2,
-        out_specs=vmem,
+        out_specs=(vmem, vmem),
         scratch_shapes=[
             pltpu.VMEM((1, BLOCKS), I32),
             pltpu.VMEM((DATES, STRIP, 2, COLS), BF16),
@@ -480,12 +518,8 @@
     )(x, owner_map)
 
 
-def finish_kernel(got_ref, linked_ref, compressed_ref, turned_ref, spread_ref):
+def finish_kernel(got_ref, spread_ref, linked_ref, compressed_ref, turned_ref):
     section = lax.axis_index("stack")
-    n, lane = iota((128, ROWS), 0), iota((128, ROWS), 1)
-    strip = ((n >> 1) & 3) * 32 + (n >> 3) * 2 + (n & 1)
-    for r in range(STRIP):
-        spread_ref[r * 128 : (r + 1) * 128] = one_hot(lane == strip * STRIP + r)
     got = jnp.concatenate([got_ref[q].astype(F32) for q in range(NZ)], axis=0)
     for tile in range(4):
         turned_ref[tile * 128 : (tile + 1) * 128] = got[:, tile * 128 : (tile + 1) * 128].T
@@ -534,7 +568,7 @@
                 compressed_ref[pl.ds(row, 1)] = mine[part][:, lanes]
 
 
-def run_finish(got):
+def run_finish(got, spread):
     vmem = pl.BlockSpec(memory_space=pltpu.VMEM)
     return pl.pallas_call(
         finish_kernel,
@@ -542,17 +576,17 @@
             jax.ShapeDtypeStruct((2 * DATES * 12, 128), F32),
             jax.ShapeDtypeStruct((24, 128), F32),
         ),
-        in_specs=[vmem],
+        in_specs=[vmem, vmem],
         out_specs=(vmem, vmem),
-        scratch_shapes=[pltpu.VMEM((512, 128), F32), pltpu.VMEM((ROWS, ROWS), BF16)],
+        scratch_shapes=[pltpu.VMEM((512, 128), F32)],
         compiler_params=pltpu.CompilerParams(vmem_limit_bytes=20 * 1024 * 1024),
         name="finish",
-    )(got)
+    )(got, spread)
 
 
 def local(slc, owner_map):
     x = jnp.transpose(slc[:, 0], (1, 2, 0, 3))
-    linked, compressed = run_finish(run_main(pltpu.with_memory_space_constraint(x, pltpu.HBM), pltpu.with_memory_space_constraint(owner_map.reshape(1, BLOCKS), pltpu.HBM)))
+    linked, compressed = run_finish(*run_main(pltpu.with_memory_space_constraint(x, pltpu.HBM), pltpu.with_memory_space_constraint(owner_map.reshape(1, BLOCKS), pltpu.HBM)))
     return (
         linked.reshape(2, 1, DATES, 1, 2 * ROWS),
         compressed.reshape(2, 1, 1, 2 * ROWS),

time: 39.8 us -> 37.7 us (0.947); the launches traced: 39 us -> 37.5 us
  Pallas kernels: 38.4 us -> 36.9 us
    pallas_call x1, Pallas kernels: 37.3 us -> 35.8 us  [run_main(): pl.pallas_call(main_kernel, out_shape=(jax.ShapeDtypeStruct((NZ, GROUPS,...]
where the time goes in v4:
time: 37.7 us; the launch traced here: 37.5 us
  Pallas kernels  36.9 us (98%)
  between operations  0.64 us (2%)
    pallas_call x1, Pallas kernels, run_main(): pl.pallas_call(main_kernel, out_shape=(jax.ShapeDtypeStruct((NZ, GROUPS,...  35.8 us
    pallas_call x1, Pallas kernels, run_finish(): pl.pallas_call(finish_kernel, out_shape=(jax.ShapeDtypeStruct((2 * DATES...  1.06 us

profile of v4, /device:TPU:6, one launch (start us, length us, event | category | flops | bytes accessed | tf_op | source)
XLA Modules:
  0.0 37.5 jit_solution(15007203264412326652)
XLA Ops:
  0.6 35.8 %link.1 = (bf16[16,8,512]{2,1,0:T(8,128)(2,1)S(1)}, bf16[768,768]{1,0:T(8,128)(2,1)S(1)}) custom-call(bf16[15,6,2,256]{3,2,1,0:T(2,128)(2,1)} %bitcast.6, s32[1,128]{1,0:T(1,128)} %bitcast.7), custom_call_target="tpu_custom_call" | custom-call | tf_op jit(solution)/shard_map/link/pallas_call | solution.py:472
  36.5 1.1 %finish.1 = (f32[360,128]{1,0:T(8,128)}, f32[24,128]{1,0:T(8,128)}) custom-call(bf16[16,8,512]{2,1,0:T(8,128)(2,1)S(1)} %get-tuple-element.6.got_ref, bf16[768,768]{1,0:T(8,128)(2,1)S(1)} %get-tuple-element.7.spread_ref), custom_call_target="tpu_custom_call" | custom-call | tf_op jit(solution)/shard_map/finish/pallas_call | solution.py:573

commit v5 on v4

--- a/solution.py
+++ b/solution.py
@@ -285,6 +285,7 @@
     slots.start()
     own = pltpu.make_async_copy(x_hbm, x_ref, sem_x.at[1])
     own.start()
+    own.wait()
     pl.semaphore_wait(barrier, len(nearest))
 
     sends = []
@@ -300,8 +301,8 @@
 
     after, before = lax.rem(me + 1, BLOCKS), lax.rem(me + BLOCKS - 1, BLOCKS)
     halos = [
-        send(x_hbm.at[:, 1:6], halo_ref.at[0], sem_hs.at[0], sem_hr.at[0], {"pix": after}),
-        send(x_hbm.at[:, 0:5], halo_ref.at[1], sem_hs.at[1], sem_hr.at[1], {"pix": before}),
+        send(x_ref.at[:, 1:6], halo_ref.at[0], sem_hs.at[0], sem_hr.at[0], {"pix": after}),
+        send(x_ref.at[:, 0:5], halo_ref.at[1], sem_hs.at[1], sem_hr.at[1], {"pix": before}),
     ]
 
     tell(sem_t.at[0], [at_x(1)])
@@ -333,16 +334,19 @@
         for part in range(2):
             v_ref[h, pl.ds((part * 16 + DATES) * 8, 8)] = jnp.zeros((8, 128), F32)
 
-    own.wait()
-    unpack(x_ref, plain, 0, STRIP)
-    for r in range(STRIP):
-        spread(plain, 0, r, UP + r, x2_ref, None)
-    middles(x2_ref, mid_ref)
     pl.semaphore_wait(sem_t.at[0], 1)
     pl.semaphore_wait(sem_t.at[1], 1)
     pl.semaphore_wait(sem_t.at[2], 2)
     tell(sem_t.at[3], [at_y(1), at_y(2), at_y(3)])
     tell(sem_t.at[4], [at_z(2), at_z(NZ - 2)])
+    unpack(x_ref, plain, 0, STRIP)
+    for r in range(STRIP):
+        spread(plain, 0, r, UP + r, x2_ref, None)
+    middles(x2_ref, mid_ref)
+    pl.semaphore_wait(sem_t.at[3], 3)
+    pl.semaphore_wait(sem_t.at[4], 2)
+    tell(sem_t.at[5], [at_core])
+    tell(sem_t.at[6], [at_z(4), at_z(NZ - 4)])
     for copy in halos:
         copy.wait_recv()
     unpack(halo_ref.at[0], plain, 1, UP)
@@ -351,10 +355,6 @@
         spread(plain, 1, r, r, x2_ref, me > 0)
         spread(plain, 2, r, UP + STRIP + r, x2_ref, me < BLOCKS - 1)
     coherences(x2_ref, mid_ref, sums_ref, band_ref, scale_ref, g_ref)
-    pl.semaphore_wait(sem_t.at[3], 3)
-    pl.semaphore_wait(sem_t.at[4], 2)
-    tell(sem_t.at[5], [at_core])
-    tell(sem_t.at[6], [at_z(4), at_z(NZ - 4)])
     power_iterations(g_ref, plain, v_ref, c_ref)
     pl.semaphore_wait(sem_t.at[5], 1)
     pl.semaphore_wait(sem_t.at[6], 2)

time: 37.7 us -> 38.4 us (1.019)
  Pallas kernels: 36.9 us -> 37.5 us
    pallas_call x1, Pallas kernels: 35.8 us -> 36.5 us  [run_main(): pl.pallas_call(main_kernel, out_shape=(jax.ShapeDtypeStruct((NZ, GROUPS,...]
where the time goes in v5:
time: 38.4 us; the launch traced here: 38.2 us
  Pallas kernels  37.5 us (98%)
  between operations  0.64 us (2%)
    pallas_call x1, Pallas kernels, run_main(): pl.pallas_call(main_kernel, out_shape=(jax.ShapeDtypeStruct((NZ, GROUPS,...  36.5 us
    pallas_call x1, Pallas kernels, run_finish(): pl.pallas_call(finish_kernel, out_shape=(jax.ShapeDtypeStruct((2 * DATES...  1.06 us

profile of v5, /device:TPU:6, one launch (start us, length us, event | category | flops | bytes accessed | tf_op | source)
XLA Modules:
  0.0 38.2 jit_solution(16098661051532408173)
XLA Ops:
  0.6 36.5 %link.1 = (bf16[16,8,512]{2,1,0:T(8,128)(2,1)S(1)}, bf16[768,768]{1,0:T(8,128)(2,1)S(1)}) custom-call(bf16[15,6,2,256]{3,2,1,0:T(2,128)(2,1)} %bitcast.6, s32[1,128]{1,0:T(1,128)} %bitcast.7), custom_call_target="tpu_custom_call" | custom-call | tf_op jit(solution)/shard_map/link/pallas_call | solution.py:472
  37.1 1.1 %finish.1 = (f32[360,128]{1,0:T(8,128)}, f32[24,128]{1,0:T(8,128)}) custom-call(bf16[16,8,512]{2,1,0:T(8,128)(2,1)S(1)} %get-tuple-element.6.got_ref, bf16[768,768]{1,0:T(8,128)(2,1)S(1)} %get-tuple-element.7.spread_ref), custom_call_target="tpu_custom_call" | custom-call | tf_op jit(solution)/shard_map/finish/pallas_call | solution.py:573
